TPU v7x, 32 devices: a whole 2x2x4 slice. The times are simulated.
32 devices in a mesh: grp: 4 (over y, x), dp: 8 (over z, core).
Axes of the slice: x: 2, y: 2, z: 4, core: 2. Of those that a mesh axis runs over, the one named last changes fastest.
Arguments:
- pixels: bfloat16 [4, 64, 256, 1024], P('grp', 'dp'), may hold values from -6 to 6
- keep_index: int32 [4, 64, 64], P('grp', 'dp'), may hold values from 0 to 255, as said below
- band_group: int32 [4, 64, 256], P('grp', 'dp'), may hold values from 0 to 3, as said below
- gsd_index: int32 [4, 64, 256], P('grp', 'dp'), may hold values from 0 to 511
- gsd_table: float32 [4, 512, 1536], P('grp'), may hold values from -4 to 4
- group_items: int32 [4], P('grp'), may hold values from 32 to 64, as said below
- step_count: int32 [1], replicated, may hold values from 2 to 20
- enc_cols: float32 [1024, 8192], P('dp'), may hold values from -0.1875 to 0.1875
- enc_rows: float32 [8192, 1024], P('dp'), may hold values from -0.09375 to 0.09375
- dec_cols: float32 [512, 4096], P('dp'), may hold values from -0.25 to 0.25
- dec_rows: float32 [4096, 512], P('dp'), may hold values from -0.1875 to 0.1875
- enc_gains: float32 [6, 1024], replicated
- dec_gains: float32 [7, 512], replicated
- moment_ecols: float32 [1024, 8192], P('dp'), may hold values from -1.5258789e-05 to 1.5258789e-05
- moment_erows: float32 [8192, 1024], P('dp'), may hold values from -1.5258789e-05 to 1.5258789e-05
- moment_dcols: float32 [512, 4096], P('dp'), may hold values from -1.5258789e-05 to 1.5258789e-05
- moment_drows: float32 [4096, 512], P('dp'), may hold values from -1.5258789e-05 to 1.5258789e-05
- moment_egains: float32 [6, 1024], replicated, may hold values from -3.0517578e-05 to 3.0517578e-05
- moment_dgains: float32 [7, 512], replicated, may hold values from -3.0517578e-05 to 3.0517578e-05
- square_ecols: float32 [1024, 8192], P('dp'), may hold values from 1.1915401e-12 to 4.7661606e-12
- square_erows: float32 [8192, 1024], P('dp'), may hold values from 1.1915401e-12 to 4.7661606e-12
- square_dcols: float32 [512, 4096], P('dp'), may hold values from 1.1915401e-12 to 4.7661606e-12
- square_drows: float32 [4096, 512], P('dp'), may hold values from 1.1915401e-12 to 4.7661606e-12
- square_egains: float32 [6, 1024], replicated, may hold values from 2.3830803e-12 to 9.532321e-12
- square_dgains: float32 [7, 512], replicated, may hold values from 2.3830803e-12 to 9.532321e-12
Outputs:
- clipped_ecols: float32 [1024, 8192], P('dp')
- squares_ecols: float32 [1024, 8192], P('dp')
- updated_ecols: float32 [1024, 8192], P('dp')
- clipped_erows: float32 [8192, 1024], P('dp')
- squares_erows: float32 [8192, 1024], P('dp')
- updated_erows: float32 [8192, 1024], P('dp')
- clipped_dcols: float32 [512, 4096], P('dp')
- squares_dcols: float32 [512, 4096], P('dp')
- updated_dcols: float32 [512, 4096], P('dp')
- clipped_drows: float32 [4096, 512], P('dp')
- squares_drows: float32 [4096, 512], P('dp')
- updated_drows: float32 [4096, 512], P('dp')
- clipped_egains: float32 [6, 1024], replicated
- squares_egains: float32 [6, 1024], replicated
- updated_egains: float32 [6, 1024], replicated
- clipped_dgains: float32 [7, 512], replicated
- squares_dgains: float32 [7, 512], replicated
- updated_dgains: float32 [7, 512], replicated
- loss: float32 [], replicated
- grad_norm: float32 [], replicated
Inputs may be any that keep to these rules, and one draw needn't show every extreme that they name: `keep_index`: each item's 64 entries are distinct patch positions. `band_group`: in groups of odd index every entry is 3. `group_items`: one group uses all 64 slots and another group 64 // 2.
All inputs are finite; a program needn't handle non-finite values.
Results may differ from a plain program's by a relative error of at most 0.017.
Values may be sent and summed in bfloat16 or wider, within the bound.
A program may use at most 384 MiB of HBM per device.

v0:
```python
import jax
import jax.numpy as jnp
from jax import lax
from jax.sharding import PartitionSpec as P

D = 1024
HEADS = 16
FF = 4096
DHEADS = 16
DFF = 2048
PIX = 1024
NBG = 4
L = 256
K = 64
norm_eps = 1e-06
clip_level = 0.005
learn_rate = 0.02
gain_rate = 0.25
weight_decay = 0.05
adam_eps = 1e-08
beta_first = 0.5
beta_second = 0.5


def to_low(value):
    return value.astype(jnp.bfloat16)


def project(inputs, matrix):
    return jnp.einsum("...n,nm->...m", inputs, matrix, preferred_element_type=jnp.float32)


def project_back(grads, matrix):
    return jnp.einsum("...m,nm->...n", grads, matrix, preferred_element_type=jnp.float32)


def weight_grad(inputs, grads):
    flat_in = inputs.reshape(-1, inputs.shape[-1])
    flat_grad = grads.reshape(-1, grads.shape[-1])
    return lax.dot_general(
        flat_in, flat_grad, (((0,), (0,)), ((), ())), preferred_element_type=jnp.float32
    )


def norm_forward(values, gain, shift):
    centred = values - jnp.mean(values, -1, keepdims=True)
    scaled = lax.rsqrt(jnp.mean(centred * centred, -1, keepdims=True) + norm_eps)
    normed = centred * scaled
    return (normed * gain + shift, normed, scaled)


def norm_backward(grads, normed, scaled, gain):
    inner = grads * gain
    back = scaled * (
        inner
        - jnp.mean(inner, -1, keepdims=True)
        - normed * jnp.mean(inner * normed, -1, keepdims=True)
    )
    flat_grad = grads.reshape(-1, grads.shape[-1])
    flat_norm = normed.reshape(-1, normed.shape[-1])
    return (back, jnp.sum(flat_grad * flat_norm, 0), jnp.sum(flat_grad, 0))


def gelu_parts(hidden):
    cumul = 0.5 * (1.0 + jax.scipy.special.erf(hidden * 0.7071067811865476))
    return (hidden * cumul, cumul + hidden * jnp.exp(-0.5 * hidden * hidden) * 0.3989422804014327)


def split_heads(packed, width, heads):
    shape = (packed.shape[0], packed.shape[1], heads, width // heads)
    return (
        packed[..., :width].reshape(shape),
        packed[..., width : 2 * width].reshape(shape),
        packed[..., 2 * width :].reshape(shape),
    )


def head_scores(queries, key_part, scale):
    return (
        jnp.einsum("bqhe,bkhe->bhqk", queries, key_part, preferred_element_type=jnp.float32) * scale
    )


def block_forward(inputs, columns, down_rows, gains, heads):
    width = inputs.shape[-1]
    scale = (width // heads) ** (-0.5)
    normed_one, hat_one, scale_one = norm_forward(inputs, gains[0], gains[1])
    first_in = to_low(normed_one)
    packed = to_low(project(first_in, columns[:, : 3 * width]))
    queries, key_part, val_part = split_heads(packed, width, heads)
    scores = head_scores(queries, key_part, scale)
    log_total = jax.nn.logsumexp(scores, -1, keepdims=True)
    attn_prob = to_low(jnp.exp(scores - log_total))
    mixed = jnp.einsum("bhqk,bkhe->bqhe", attn_prob, val_part, preferred_element_type=jnp.float32)
    mixed = to_low(mixed.reshape(inputs.shape))
    middle = inputs + project(mixed, columns[:, 3 * width : 4 * width])
    normed_two, hat_two, scale_two = norm_forward(middle, gains[2], gains[3])
    second_in = to_low(normed_two)
    hidden = project(second_in, columns[:, 4 * width :])
    activated = to_low(gelu_parts(hidden)[0])
    output = middle + project(activated, down_rows)
    saved = (
        hat_one,
        scale_one,
        first_in,
        packed,
        log_total,
        mixed,
        hat_two,
        scale_two,
        second_in,
        hidden,
        activated,
    )
    return (output, saved)


def block_backward(grad_out, columns, down_rows, gains, heads, saved):
    (
        hat_one,
        scale_one,
        first_in,
        packed,
        log_total,
        mixed,
        hat_two,
        scale_two,
        second_in,
        hidden,
        activated,
    ) = saved
    width = grad_out.shape[-1]
    scale = (width // heads) ** (-0.5)
    grad_low = to_low(grad_out)
    grad_down = weight_grad(activated, grad_low)
    grad_hidden = to_low(project_back(grad_low, down_rows) * gelu_parts(hidden)[1])
    grad_up = weight_grad(second_in, grad_hidden)
    back_two, gain_two, shift_two = norm_backward(
        project_back(grad_hidden, columns[:, 4 * width :]), hat_two, scale_two, gains[2]
    )
    grad_middle = grad_out + back_two
    middle_low = to_low(grad_middle)
    grad_proj = weight_grad(mixed, middle_low)
    head_shape = packed.shape[:2] + (heads, width // heads)
    grad_mixed = to_low(
        project_back(middle_low, columns[:, 3 * width : 4 * width]).reshape(head_shape)
    )
    queries, key_part, val_part = split_heads(packed, width, heads)
    attn_prob = jnp.exp(head_scores(queries, key_part, scale) - log_total)
    grad_prob = jnp.einsum(
        "bqhe,bkhe->bhqk", grad_mixed, val_part, preferred_element_type=jnp.float32
    )
    grad_val = jnp.einsum(
        "bhqk,bqhe->bkhe", to_low(attn_prob), grad_mixed, preferred_element_type=jnp.float32
    )
    grad_score = to_low(attn_prob * (grad_prob - jnp.sum(grad_prob * attn_prob, -1, keepdims=True)))
    grad_query = (
        jnp.einsum("bhqk,bkhe->bqhe", grad_score, key_part, preferred_element_type=jnp.float32)
        * scale
    )
    grad_key = (
        jnp.einsum("bhqk,bqhe->bkhe", grad_score, queries, preferred_element_type=jnp.float32)
        * scale
    )
    flat_shape = packed.shape[:2] + (width,)
    grad_packed = to_low(
        jnp.concatenate(
            [
                grad_query.reshape(flat_shape),
                grad_key.reshape(flat_shape),
                grad_val.reshape(flat_shape),
            ],
            -1,
        )
    )
    grad_qkv = weight_grad(first_in, grad_packed)
    back_one, gain_one, shift_one = norm_backward(
        project_back(grad_packed, columns[:, : 3 * width]), hat_one, scale_one, gains[0]
    )
    grad_in = grad_middle + back_one
    grad_cols = jnp.concatenate([grad_qkv, grad_proj, grad_up], 1)
    grad_gains = jnp.stack([gain_one, shift_one, gain_two, shift_two])
    return (grad_in, grad_cols, grad_down, grad_gains)


def adam_step(master, moment, square, grad, factor, fix_one, fix_two, decay, rate):
    clipped = grad * factor
    moment_new = beta_first * moment + (1.0 - beta_first) * clipped
    square_new = beta_second * square + (1.0 - beta_second) * clipped * clipped
    direction = moment_new / fix_one / (jnp.sqrt(square_new / fix_two) + adam_eps) + decay * master
    return (clipped, square_new, master - rate * direction)


def body(
    pixels,
    keep_index,
    band_group,
    gsd_index,
    gsd_table,
    group_items,
    step_count,
    enc_cols,
    enc_rows,
    dec_cols,
    dec_rows,
    enc_gains,
    dec_gains,
    moment_ecols,
    moment_erows,
    moment_dcols,
    moment_drows,
    moment_egains,
    moment_dgains,
    square_ecols,
    square_erows,
    square_dcols,
    square_drows,
    square_egains,
    square_dgains,
):
    total_count = lax.psum(jnp.sum(group_items.astype(jnp.float32)), "grp")
    masked = total_count * (L - K)
    copies = (
        lax.all_gather(to_low(enc_cols), "dp", axis=0, tiled=True),
        lax.all_gather(to_low(enc_rows), "dp", axis=0, tiled=True),
        lax.all_gather(to_low(dec_cols), "dp", axis=0, tiled=True),
        lax.all_gather(to_low(dec_rows), "dp", axis=0, tiled=True),
    )
    enc_copy = copies[0]
    enc_down = copies[1][:FF]
    embed_w = copies[1][FF:]
    dec_copy = copies[2]
    dec_down = copies[3][:DFF]
    dec_embed = copies[3][DFF : DFF + D]
    head_rows = copies[3][DFF + D :]
    pixel_rows = pixels[0]
    keep_rows = keep_index[0]
    batch = pixel_rows.shape[0]
    kept_pixels = jnp.take_along_axis(pixel_rows, keep_rows[..., None], 1)
    kept_bands = jnp.take_along_axis(band_group[0], keep_rows, 1)
    onehot = (kept_bands[..., None] == jnp.arange(NBG, dtype=jnp.int32)).astype(jnp.bfloat16)
    spread = (onehot[..., None] * kept_pixels[:, :, None, :]).reshape(batch, K, NBG * PIX)
    position = jnp.take(gsd_table[0], gsd_index[0], axis=0)
    enc_input = project(spread, embed_w) + jnp.take_along_axis(
        position[..., :D], keep_rows[..., None], 1
    )
    enc_out, enc_saved = block_forward(enc_input, enc_copy, enc_down, enc_gains, HEADS)
    enc_final, enc_hat, enc_scale = norm_forward(enc_out, enc_gains[4], enc_gains[5])
    enc_low = to_low(enc_final)
    latent = project(enc_low, dec_embed)
    item_rows = jnp.arange(batch)[:, None]
    hidden_mask = jnp.ones((batch, L), jnp.float32).at[item_rows, keep_rows].set(0.0)
    dec_input = hidden_mask[..., None] * dec_gains[6] + position[..., D:]
    dec_input = dec_input.at[item_rows, keep_rows].add(latent)
    dec_out, dec_saved = block_forward(dec_input, dec_copy, dec_down, dec_gains, DHEADS)
    dec_final, dec_hat, dec_scale = norm_forward(dec_out, dec_gains[4], dec_gains[5])
    dec_low = to_low(dec_final)
    predicted = project_back(dec_low, head_rows)
    pixel_float = pixel_rows.astype(jnp.float32)
    centred = pixel_float - jnp.mean(pixel_float, -1, keepdims=True)
    target = centred * lax.rsqrt(jnp.mean(centred * centred, -1, keepdims=True) + norm_eps)
    first_item = lax.axis_index("dp") * batch
    valid = (first_item + jnp.arange(batch, dtype=jnp.int32) < group_items[0]).astype(jnp.float32)
    token_weight = hidden_mask * valid[:, None]
    error = predicted - target
    loss_local = jnp.sum(token_weight * jnp.mean(error * error, -1))
    grad_pred = to_low(token_weight[..., None] * error * (2.0 / PIX) / masked)
    grad_head = weight_grad(grad_pred, dec_low)
    back_dec, gain_df, shift_df = norm_backward(
        project(grad_pred, head_rows), dec_hat, dec_scale, dec_gains[4]
    )
    grad_dec_in, grad_dcols, grad_ddown, dec_block_gains = block_backward(
        back_dec, dec_copy, dec_down, dec_gains, DHEADS, dec_saved
    )
    grad_token = jnp.sum(grad_dec_in * hidden_mask[..., None], (0, 1))
    grad_latent = to_low(jnp.take_along_axis(grad_dec_in, keep_rows[..., None], 1))
    grad_dembed = weight_grad(enc_low, grad_latent)
    back_enc, gain_ef, shift_ef = norm_backward(
        project_back(grad_latent, dec_embed), enc_hat, enc_scale, enc_gains[4]
    )
    grad_enc_in, grad_ecols, grad_edown, enc_block_gains = block_backward(
        back_enc, enc_copy, enc_down, enc_gains, HEADS, enc_saved
    )
    grad_embed = weight_grad(spread, to_low(grad_enc_in))
    grads = (
        grad_ecols,
        jnp.concatenate([grad_edown, grad_embed], 0),
        grad_dcols,
        jnp.concatenate([grad_ddown, grad_dembed, grad_head], 0),
    )
    grad_egains = jnp.concatenate([enc_block_gains, jnp.stack([gain_ef, shift_ef])], 0)
    grad_dgains = jnp.concatenate([dec_block_gains, jnp.stack([gain_df, shift_df, grad_token])], 0)
    shards = (
        lax.psum_scatter(grads[0], "dp", scatter_dimension=0, tiled=True),
        lax.psum_scatter(grads[1], "dp", scatter_dimension=0, tiled=True),
        lax.psum_scatter(grads[2], "dp", scatter_dimension=0, tiled=True),
        lax.psum_scatter(grads[3], "dp", scatter_dimension=0, tiled=True),
    )
    shards = (
        lax.psum(shards[0].astype(jnp.bfloat16), "grp").astype(jnp.float32),
        lax.psum(shards[1].astype(jnp.bfloat16), "grp").astype(jnp.float32),
        lax.psum(shards[2].astype(jnp.bfloat16), "grp").astype(jnp.float32),
        lax.psum(shards[3].astype(jnp.bfloat16), "grp").astype(jnp.float32),
    )
    enc_sum, dec_sum, loss_sum = lax.psum((grad_egains, grad_dgains, loss_local), ("grp", "dp"))
    shard_squares = lax.psum(sum((jnp.sum(piece * piece) for piece in shards)), "dp")
    loss = loss_sum / masked
    grad_norm = jnp.sqrt(shard_squares + jnp.sum(enc_sum * enc_sum) + jnp.sum(dec_sum * dec_sum))
    factor = clip_level / jnp.maximum(grad_norm, clip_level)
    count_steps = step_count[0].astype(jnp.float32)
    fix_one = 1.0 - beta_first**count_steps
    fix_two = 1.0 - beta_second**count_steps
    clipped_ecols, squares_ecols, updated_ecols = adam_step(
        enc_cols,
        moment_ecols,
        square_ecols,
        shards[0],
        factor,
        fix_one,
        fix_two,
        weight_decay,
        learn_rate,
    )
    clipped_erows, squares_erows, updated_erows = adam_step(
        enc_rows,
        moment_erows,
        square_erows,
        shards[1],
        factor,
        fix_one,
        fix_two,
        weight_decay,
        learn_rate,
    )
    clipped_dcols, squares_dcols, updated_dcols = adam_step(
        dec_cols,
        moment_dcols,
        square_dcols,
        shards[2],
        factor,
        fix_one,
        fix_two,
        weight_decay,
        learn_rate,
    )
    clipped_drows, squares_drows, updated_drows = adam_step(
        dec_rows,
        moment_drows,
        square_drows,
        shards[3],
        factor,
        fix_one,
        fix_two,
        weight_decay,
        learn_rate,
    )
    clipped_egains, squares_egains, updated_egains = adam_step(
        enc_gains, moment_egains, square_egains, enc_sum, factor, fix_one, fix_two, 0.0, gain_rate
    )
    clipped_dgains, squares_dgains, updated_dgains = adam_step(
        dec_gains, moment_dgains, square_dgains, dec_sum, factor, fix_one, fix_two, 0.0, gain_rate
    )
    return (
        clipped_ecols,
        squares_ecols,
        updated_ecols,
        clipped_erows,
        squares_erows,
        updated_erows,
        clipped_dcols,
        squares_dcols,
        updated_dcols,
        clipped_drows,
        squares_drows,
        updated_drows,
        clipped_egains,
        squares_egains,
        updated_egains,
        clipped_dgains,
        squares_dgains,
        updated_dgains,
        loss,
        grad_norm,
    )


def solution(mesh):
    return jax.shard_map(
        body,
        mesh=mesh,
        in_specs=(
            P("grp", "dp", None, None),
            P("grp", "dp", None),
            P("grp", "dp", None),
            P("grp", "dp", None),
            P("grp", None, None),
            P("grp"),
            P(),
            P("dp", None),
            P("dp", None),
            P("dp", None),
            P("dp", None),
            P(),
            P(),
            P("dp", None),
            P("dp", None),
            P("dp", None),
            P("dp", None),
            P(),
            P(),
            P("dp", None),
            P("dp", None),
            P("dp", None),
            P("dp", None),
            P(),
            P(),
        ),
        out_specs=(
            P("dp", None),
            P("dp", None),
            P("dp", None),
            P("dp", None),
            P("dp", None),
            P("dp", None),
            P("dp", None),
            P("dp", None),
            P("dp", None),
            P("dp", None),
            P("dp", None),
            P("dp", None),
            P(),
            P(),
            P(),
            P(),
            P(),
            P(),
            P(),
            P(),
        ),
        check_vma=False,
    )
```

profile of v0, /device:TPU:0, one launch (start us, length us, event | category | flops | bytes accessed | tf_op | source)
XLA Modules:
  0.0 1718.9 jit_solution(14711521115183976709)
XLA Ops:
  7.3 4.0 convert_element_type.164
  20.2 12.5 psum.63
  43.0 10.9 gather_fusion.2
  59.1 7.8 mul.696
  66.9 11.0 gather_fusion
  77.9 10.1 broadcast_select_fusion
  88.0 8.4 slice.161
  96.4 10.5 gather_fusion.3
  108.0 24.3 %scatter_fusion = f32[8,256]{1,0:T(8,128)S(1)} fusion(f32[8,256]{1,0:T(8,128)S(1)} %broadcast_in_dim.52, s32[512]{0:T(512)S(1)} %reshape.496, f32[512]{0:T(512)S(1)} %broadcast.507), kind=kCustom, calls=%fused_computation.5 | custom fusion | bytes 10240 | tf_op jit(solution)/shard_map/scatter | solution.py:252
  132.4 4.6 slice_add_fusion
  137.0 28.3 %all-gather.5.cloned.1.call-done = bf16[8192,1024]{1,0:T(8,128)(2,1)} async-done(((bf16[1024,1024]{1,0:T(8,128)(2,1)}), bf16[8192,1024]{1,0:T(8,128)(2,1)}) %all-gather.5.cloned.1.call-update) | async-done | bytes 16777232 | tf_op jit(solution)/shard_map/all_gather | solution.py:225
  165.2 9.7 fusion.120
  175.4 141.4 %all-gather.7.cloned.1.call-done = bf16[1024,8192]{1,0:T(8,128)(2,1)} async-done(((bf16[128,8192]{1,0:T(8,128)(2,1)}), bf16[1024,8192]{1,0:T(8,128)(2,1)}) %all-gather.7.cloned.1.call-update) | async-done | bytes 16777232 | tf_op jit(solution)/shard_map/all_gather | solution.py:224
  316.8 6.6 fusion.23
  328.0 4.0 reshape.453
  346.2 10.8 multiply_convert_fusion.2
  358.0 4.6 fusion.122
  366.3 64.7 %scatter_fusion.1 = f32[8,256,512]{2,1,0:T(8,128)} fusion(f32[8,256,512]{2,1,0:T(8,128)} %slice_add_fusion, s32[512]{0:T(512)S(1)} %reshape.496, f32[512,512]{1,0:T(8,128)S(1)} %bitcast.272), kind=kCustom, calls=%fused_computation.6 | custom fusion | flops 262144 | bytes 3149824 | tf_op jit(solution)/shard_map/scatter-add | solution.py:254
  437.1 6.3 convolution_convert_fusion
  451.4 4.5 copy.91
  455.9 14.4 multiply_reduce_fusion.1
  470.3 13.8 exponential_reduce_fusion
  484.2 15.7 fusion.42
  499.9 4.4 fusion.123
  506.5 9.3 multiply_convert_fusion.1
  515.9 4.6 fusion.124
  528.5 6.9 divide_convert_fusion
  535.4 6.6 multiply_reduce_fusion.4
  544.2 13.8 fusion.6
  558.0 7.1 convolution_bitcast_fusion.5
  565.1 6.7 multiply_reduce_fusion.5
  578.5 3.9 copy.96
  582.5 15.9 fusion.45
  598.4 23.3 %multiply_reduce_fusion = (f32[8,16,256]{2,1,0:T(8,128)S(1)}, f32[8,16,256,256]{2,3,1,0:T(8,128)}) fusion(f32[8,16,256,256]{2,3,1,0:T(8,128)} %get-tuple-element.107, f32[8,16,256]{2,1,0:T(8,128)S(1)} %log_add_fusion, bf16[8,256,16,32]{1,3,2,0:T(8,128)(2,1)} %bitcast.251, bf16[8,256,16,32]{1,3,2,0:T(8,128)(2,1)S(1)} %bitcast.249), kind=kOutput, calls=%fused_computation.10 | convolution fusion | flops 570392576 | bytes 71565312 | tf_op jit(solution)/shard_map/bqhe,bkhe->bhqk/dot_general | solution.py:150
  621.7 28.0 %multiply_convert_fusion = bf16[8,16,256,256]{2,3,1,0:T(8,128)(2,1)} fusion(f32[8,16,256,256]{2,3,1,0:T(8,128)} %get-tuple-element.119, f32[8,16,256,256]{2,3,1,0:T(8,128)} %get-tuple-element.107, f32[8,16,256]{2,1,0:T(8,128)S(1)} %get-tuple-element.118, f32[8,16,256]{2,1,0:T(8,128)S(1)} %log_add_fusion), kind=kLoop, calls=%fused_computation.9 | loop fusion | flops 41943040 | bytes 84148224 | tf_op jit(solution)/shard_map/convert_element_type | solution.py:26
  649.7 12.0 multiply_convert_fusion.6
  661.7 10.5 multiply_convert_fusion.7
  672.3 4.1 copy.102
  676.4 3.9 copy.100
  682.8 7.8 convolution_bitcast_fusion.3
  695.9 8.2 multiply_reduce_fusion.6
  718.8 4.6 convolution_bitcast_fusion.4
  732.6 11.0 fusion.16
  743.7 9.7 multiply_reduce_fusion.19
  760.1 5.5 convolution_convert_fusion.1
  767.8 4.6 multiply_reduce_fusion.7
  778.0 4.1 reshape.460
  788.7 6.1 convolution_bitcast_fusion.6
  794.9 7.0 convolution_bitcast_fusion.2
  801.9 8.6 convolution_bitcast_fusion.1
  810.5 22.9 %pad_maximum_fusion = f32[1024,8192]{1,0:T(8,128)} fusion(f32[1024,4096]{1,0:T(8,128)} %convolution_bitcast_fusion.1, f32[1024,1024]{1,0:T(8,128)} %convolution_bitcast_fusion.6, f32[1024,3072]{1,0:T(8,128)} %convolution_bitcast_fusion.2), kind=kLoop, calls=%fused_computation.7 | loop fusion | flops 16777216 | bytes 67108864 | tf_op jit(solution)/shard_map/concatenate | solution.py:181
  833.7 4.6 copy.152
  838.3 6.9 multiply_reduce_fusion.20
  846.0 4.7 fusion.125
  850.7 8.8 convolution_bitcast_fusion
  859.5 18.8 %pad_maximum_fusion.1 = f32[8192,1024]{1,0:T(8,128)} fusion(f32[4096,1024]{1,0:T(8,128)S(1)} %fusion.125, f32[4096,1024]{1,0:T(8,128)} %convolution_bitcast_fusion), kind=kLoop, calls=%fused_computation.8 | loop fusion | flops 8388608 | bytes 67108864 | tf_op jit(solution)/shard_map/concatenate | solution.py:287
  882.7 316.6 %reduce-scatter.5.cloned.1.call-done = f32[128,8192]{1,0:T(8,128)} async-done(((f32[1024,8192]{1,0:T(8,128)}), f32[128,8192]{1,0:T(8,128)}) %reduce-scatter.5.cloned.1.call-update) | async-done | bytes 4194320 | tf_op jit(solution)/shard_map/reduce_scatter | solution.py:294
  1203.0 322.7 %reduce-scatter.7.cloned.1.call-done = f32[1024,1024]{1,0:T(8,128)} async-done(((f32[8192,1024]{1,0:T(8,128)}), f32[1024,1024]{1,0:T(8,128)}) %reduce-scatter.7.cloned.1.call-update) | async-done | bytes 4194320 | tf_op jit(solution)/shard_map/reduce_scatter | solution.py:295
  1530.7 38.8 %all-reduce = (f32[6,1024]{1,0:T(8,128)S(1)}, f32[7,512]{1,0:T(8,128)S(1)}, f32[]{:T(128)}) all-reduce(f32[6,1024]{1,0:T(8,128)S(1)} %concatenate.37, f32[7,512]{1,0:T(8,128)S(1)} %concatenate.38, f32[]{:T(128)} %get-tuple-element.69), channel_id=1, replica_groups=mesh['grp'=4,'dp'=8] {'grp','dp'}, use_global_device_ids=true, to_apply=%region_54.55 | all-reduce | flops 9729 | bytes 77832 | tf_op jit(solution)/shard_map/psum | solution.py:305
  1570.7 81.2 %all-reduce.4.cloned.1.call-done = (bf16[128,8192]{1,0:T(8,128)(2,1)}, bf16[1024,1024]{1,0:T(8,128)(2,1)}, bf16[64,4096]{1,0:T(8,128)(2,1)}, bf16[512,512]{1,0:T(8,128)(2,1)}) async-done(((bf16[128,8192]{1,0:T(8,128)(2,1)}, bf16[1024,1024]{1,0:T(8,128)(2,1)}, bf16[64,4096]{1,0:T(8,128)(2,1)}, bf16[512,512]{1,0:T(8,128)(2,1)}), (bf16[128,8192]{1,0:T(8,128)(2,1)}, bf16[1024,1024]{1,0:T(8,128)(2,1)}, ...) | async-done | bytes 5242896 | tf_op jit(solution)/shard_map/psum | solution.py:300
  1664.1 17.0 psum.68
  1688.4 4.2 fusion.64
  1693.5 8.9 fusion.35
  1704.3 5.6 fusion.30
  (419 shorter events, 164.3 us)
Async XLA Ops:
  7.2 59.7 %copy-start = (f32[1,512,1536]{2,1,0:T(8,128)S(1)}, f32[1,512,1536]{2,1,0:T(8,128)}, u32[]{:S(2)}) copy-start(f32[1,512,1536]{2,1,0:T(8,128)} %param.29) | copy-start | bytes 9437188
  7.2 158.0 %all-gather.5.cloned.1.call-start = ((), (), s32[]{:S(2)}) async-start(), calls=%async_computation.4 | async-start | bytes 18874368 | tf_op jit(solution)/shard_map/all_gather | solution.py:225
  11.3 305.5 %all-gather.7.cloned.1.call-start = ((), (), s32[]{:S(2)}) async-start(), calls=%async_computation.5 | async-start | bytes 18874368 | tf_op jit(solution)/shard_map/all_gather | solution.py:224
  15.1 349.2 %all-gather.9.cloned.1.call-start = ((), (), s32[]{:S(2)}) async-start(), calls=%async_computation.6 | async-start | bytes 4718592 | tf_op jit(solution)/shard_map/all_gather | solution.py:227
  17.3 419.3 %all-gather.11.cloned.1.call-start = ((), (), s32[]{:S(2)}) async-start(), calls=%async_computation.7 | async-start | bytes 4718592 | tf_op jit(solution)/shard_map/all_gather | solution.py:226
  19.4 859.0 %reduce-scatter.9.cloned.1.call-start = ((), (), s32[]{:S(2)}) async-start(), calls=%async_computation.10 | async-start | bytes 9437184 | tf_op jit(solution)/shard_map/reduce_scatter | solution.py:296
  38.4 57.9 %copy-start.6 = (s32[512]{0:T(512)}, s32[512]{0:T(512)S(1)}, u32[]{:S(2)}) copy-start(s32[512]{0:T(512)S(1)} %reshape.472) | copy-start | bytes 6148
  42.1 123.1 %copy-start.108 = (pred[8,64]{1,0:T(8,128)(4,1)}, pred[8,64]{1,0:T(8,128)(4,1)S(1)}, u32[]{:S(2)}) copy-start(pred[8,64]{1,0:T(8,128)(4,1)S(1)} %get-tuple-element.74) | copy-start | bytes 1540
  42.7 393.8 %copy-start.105 = (f32[1,512]{1,0:T(1,128)}, f32[1,512]{1,0:T(1,128)S(1)}, u32[]{:S(2)}) copy-start(f32[1,512]{1,0:T(1,128)S(1)} %get-tuple-element.91) | copy-start | bytes 6148
  42.7 393.8 %copy-start.120 = (f32[1,512]{1,0:T(1,128)}, f32[1,512]{1,0:T(1,128)S(1)}, u32[]{:S(2)}) copy-start(f32[1,512]{1,0:T(1,128)S(1)} %get-tuple-element.90) | copy-start | bytes 6148
  42.8 274.0 %copy-start.61 = (f32[1,1024]{1,0:T(1,128)}, f32[1,1024]{1,0:T(1,128)S(1)}, u32[]{:S(2)}) copy-start(f32[1,1024]{1,0:T(1,128)S(1)} %get-tuple-element.85) | copy-start | bytes 12292
  42.8 274.0 %copy-start.65 = (f32[1,1024]{1,0:T(1,128)}, f32[1,1024]{1,0:T(1,128)S(1)}, u32[]{:S(2)}) copy-start(f32[1,1024]{1,0:T(1,128)S(1)} %get-tuple-element.84) | copy-start | bytes 12292
  42.8 303.4 %copy-start.92 = (f32[1,1024]{1,0:T(1,128)}, f32[1,1024]{1,0:T(1,128)S(1)}, u32[]{:S(2)}) copy-start(f32[1,1024]{1,0:T(1,128)S(1)} %get-tuple-element.83) | copy-start | bytes 12292
  42.8 303.4 %copy-start.114 = (f32[1,1024]{1,0:T(1,128)}, f32[1,1024]{1,0:T(1,128)S(1)}, u32[]{:S(2)}) copy-start(f32[1,1024]{1,0:T(1,128)S(1)} %get-tuple-element.82) | copy-start | bytes 12292
  42.8 321.5 %copy-start.99 = (f32[1,1024]{1,0:T(1,128)}, f32[1,1024]{1,0:T(1,128)S(1)}, u32[]{:S(2)}) copy-start(f32[1,1024]{1,0:T(1,128)S(1)} %get-tuple-element.81) | copy-start | bytes 12292
  42.8 321.5 %copy-start.116 = (f32[1,1024]{1,0:T(1,128)}, f32[1,1024]{1,0:T(1,128)S(1)}, u32[]{:S(2)}) copy-start(f32[1,1024]{1,0:T(1,128)S(1)} %get-tuple-element.86) | copy-start | bytes 12292
  175.0 167.1 %copy-start.17 = (f32[8,64,1024]{2,1,0:T(8,128)}, f32[8,64,1024]{2,1,0:T(8,128)S(1)}, u32[]{:S(2)}) copy-start(f32[8,64,1024]{2,1,0:T(8,128)S(1)} %get-tuple-element.97) | copy-start | bytes 6291460
  175.0 148.4 %copy-start.59 = (f32[8,64]{1,0:T(8,128)}, f32[8,64]{1,0:T(8,128)S(1)}, u32[]{:S(2)}) copy-start(f32[8,64]{1,0:T(8,128)S(1)} %broadcast_multiply_fusion.22) | copy-start | bytes 6148
  175.4 148.0 %copy-start.63 = (f32[8,64]{1,0:T(8,128)}, f32[8,64]{1,0:T(8,128)S(1)}, u32[]{:S(2)}) copy-start(f32[8,64]{1,0:T(8,128)S(1)} %add_rsqrt_fusion.6) | copy-start | bytes 6148
  345.8 11.3 copy-start.23
  345.8 11.3 copy-start.78
  345.8 11.3 slice-start
  346.2 10.9 copy-start.94
  346.2 10.9 slice-start.1
  346.2 10.9 slice-start.2
  346.2 11.8 slice-start.3
  362.6 68.4 %copy-start.37 = (f32[8,64,1024]{2,1,0:T(8,128)}, f32[8,64,1024]{2,1,0:T(8,128)S(1)}, u32[]{:S(2)}) copy-start(f32[8,64,1024]{2,1,0:T(8,128)S(1)} %get-tuple-element.105) | copy-start | bytes 6291460
  362.6 68.4 %copy-start.80 = (f32[8,64]{1,0:T(8,128)}, f32[8,64]{1,0:T(8,128)S(1)}, u32[]{:S(2)}) copy-start(f32[8,64]{1,0:T(8,128)S(1)} %broadcast_multiply_fusion.20) | copy-start | bytes 6148
  363.0 68.0 %copy-start.101 = (f32[8,64]{1,0:T(8,128)}, f32[8,64]{1,0:T(8,128)S(1)}, u32[]{:S(2)}) copy-start(f32[8,64]{1,0:T(8,128)S(1)} %add_rsqrt_fusion.4) | copy-start | bytes 6148
  451.3 18.9 %copy-start.13 = (bf16[8,256,512]{1,2,0:T(8,128)(2,1)}, bf16[8,256,512]{1,2,0:T(8,128)(2,1)S(1)}, u32[]{:S(2)}) copy-start(bf16[8,256,512]{1,2,0:T(8,128)(2,1)S(1)} %copy.92) | copy-start | bytes 6291460
  470.3 13.9 copy-start.19
  506.5 9.4 copy-start.129
  520.5 21.4 %copy-start.28 = (f32[8,256,512]{2,1,0:T(8,128)}, f32[8,256,512]{2,1,0:T(8,128)S(1)}, u32[]{:S(2)}) copy-start(f32[8,256,512]{2,1,0:T(8,128)S(1)} %get-tuple-element.113) | copy-start | bytes 12582916
  520.6 21.4 %copy-start.74 = (f32[8,256]{1,0:T(8,128)}, f32[8,256]{1,0:T(8,128)S(1)}, u32[]{:S(2)}) copy-start(f32[8,256]{1,0:T(8,128)S(1)} %broadcast_multiply_fusion.11) | copy-start | bytes 24580
  521.4 20.6 %copy-start.88 = (f32[8,256]{1,0:T(8,128)}, f32[8,256]{1,0:T(8,128)S(1)}, u32[]{:S(2)}) copy-start(f32[8,256]{1,0:T(8,128)S(1)} %add_rsqrt_fusion.1) | copy-start | bytes 24580
  543.5 28.3 %copy-start.26 = (f32[8,256,512]{2,1,0:T(8,128)}, f32[8,256,512]{2,1,0:T(8,128)S(1)}, u32[]{:S(2)}) copy-start(f32[8,256,512]{2,1,0:T(8,128)S(1)} %subtract_multiply_fusion) | copy-start | bytes 12582916
  621.7 28.0 %copy-start.14 = (bf16[8,256,512]{1,2,0:T(8,128)(2,1)S(1)}, bf16[8,256,512]{1,2,0:T(8,128)(2,1)}, u32[]{:S(2)}) copy-start(bf16[8,256,512]{1,2,0:T(8,128)(2,1)} %copy-done.13) | copy-start | bytes 6291460
  672.3 8.0 copy-start.33
  682.8 7.8 copy-start.32
  694.3 9.8 copy-start.4
  694.3 186.2 %reduce-scatter.11.cloned.1.call-start = ((), (), s32[]{:S(2)}) async-start(), calls=%async_computation.11 | async-start | bytes 9437184 | tf_op jit(solution)/shard_map/reduce_scatter | solution.py:297
  695.9 8.3 copy-start.8
  695.9 8.3 copy-start.16
  727.3 471.9 %reduce-scatter.5.cloned.1.call-start = ((), (), s32[]{:S(2)}) async-start(), calls=%async_computation.8 | async-start | bytes 37748736 | tf_op jit(solution)/shard_map/reduce_scatter | solution.py:294
  732.5 20.9 %copy-start.40 = (f32[8,64,1024]{2,1,0:T(8,128)}, f32[8,64,1024]{2,1,0:T(8,128)S(1)}, u32[]{:S(2)}) copy-start(f32[8,64,1024]{2,1,0:T(8,128)S(1)} %subtract_multiply_fusion.4) | copy-start | bytes 6291460
  732.5 11.1 copy-start.24
  732.6 11.1 copy-start.79
  732.6 11.1 copy-start.93
  732.6 11.1 copy-start.95
  743.7 9.7 copy-start.134
  833.4 692.2 %reduce-scatter.7.cloned.1.call-start = ((), (), s32[]{:S(2)}) async-start(), calls=%async_computation.9 | async-start | bytes 37748736 | tf_op jit(solution)/shard_map/reduce_scatter | solution.py:295
  878.3 773.6 %all-reduce.4.cloned.1.call-start = ((), (), s32[]{:S(2)}) async-start(), calls=%async_computation.12 | async-start | bytes 10485760 | tf_op jit(solution)/shard_map/psum | solution.py:300
  1529.6 153.6 %copy-start.77 = (f32[7,512]{1,0:T(8,128)S(1)}, f32[7,512]{1,0:T(8,128)}, u32[]{:S(2)}) copy-start(f32[7,512]{1,0:T(8,128)} %param.37) | copy-start | bytes 43012
  1529.6 153.6 %copy-start.96 = (f32[7,512]{1,0:T(8,128)S(1)}, f32[7,512]{1,0:T(8,128)}, u32[]{:S(2)}) copy-start(f32[7,512]{1,0:T(8,128)} %param.43) | copy-start | bytes 43012
  1529.6 153.6 %copy-start.97 = (f32[7,512]{1,0:T(8,128)S(1)}, f32[7,512]{1,0:T(8,128)}, u32[]{:S(2)}) copy-start(f32[7,512]{1,0:T(8,128)} %param.49) | copy-start | bytes 43012
  1529.6 154.2 %copy-start.69 = (f32[6,1024]{1,0:T(8,128)S(1)}, f32[6,1024]{1,0:T(8,128)}, u32[]{:S(2)}) copy-start(f32[6,1024]{1,0:T(8,128)} %param.36) | copy-start | bytes 73732
  1529.6 154.2 %copy-start.85 = (f32[6,1024]{1,0:T(8,128)S(1)}, f32[6,1024]{1,0:T(8,128)}, u32[]{:S(2)}) copy-start(f32[6,1024]{1,0:T(8,128)} %param.42) | copy-start | bytes 73732
  1529.6 154.2 %copy-start.86 = (f32[6,1024]{1,0:T(8,128)S(1)}, f32[6,1024]{1,0:T(8,128)}, u32[]{:S(2)}) copy-start(f32[6,1024]{1,0:T(8,128)} %param.48) | copy-start | bytes 73732
  1529.7 154.8 %copy-start.49 = (f32[512,512]{1,0:T(8,128)S(1)}, f32[512,512]{1,0:T(8,128)}, u32[]{:S(2)}) copy-start(f32[512,512]{1,0:T(8,128)} %param.35) | copy-start | bytes 3145732
  1684.5 8.1 copy-start.50
  1693.5 8.9 copy-start.31
  1693.5 8.9 copy-start.43
  1693.5 9.1 copy-start.51
  1693.5 10.8 copy-start.52
  (87 other events, 348.9 us)
Sparse Core Ops, SparseCore 0:
  11.4 153.7 all-gather.4
  167.4 149.3 all-gather.6
  318.9 45.3 all-gather.8
  366.4 45.8 all-gather.10
  694.4 88.3 reduce-scatter.8
  784.9 87.9 reduce-scatter.10
  875.3 323.8 reduce-scatter.4
  1201.7 323.8 reduce-scatter.6
  1530.6 121.2 all-reduce.3
where the time goes:
time: 1730 us; the launch traced here: 1720 us
  waiting for transfers between devices  892 us (52%)
  matrix products  310 us (18%)
  other arithmetic  265 us (15%)
  local copies, waits for them, and re-layouts  157 us (9%)
  blocking collectives  68.3 us (4%)
  between operations  25.6 us (1%)
    reduce_scatter x1, waiting for transfers between devices, body(): lax.psum_scatter(grads[1], 'dp', scatter_dimension=0, tiled=True)  323 us
    reduce_scatter x1, waiting for transfers between devices, body(): lax.psum_scatter(grads[0], 'dp', scatter_dimension=0, tiled=True)  317 us
    all_gather x1, waiting for transfers between devices, body(): lax.all_gather(to_low(enc_cols), 'dp', axis=0, tiled=True)  141 us
    psum x1, waiting for transfers between devices, body(): lax.psum(shards[0].astype(jnp.bfloat16), 'grp').astype(jnp.float32)  81.2 us
    dot_general x11, matrix products, project(): jnp.einsum('...n,nm->...m', inputs, matrix, preferred_element_type=jnp.fl...  68.6 us
    dot_general x10, matrix products, project_back(): jnp.einsum('...m,nm->...n', grads, matrix, preferred_element_type=jnp.flo...  68.4 us
    scatter-add x1, other arithmetic, body(): dec_input = dec_input.at[item_rows, keep_rows].add(latent)  64.7 us
    dot_general x11, matrix products, weight_grad(): lax.dot_general(flat_in, flat_grad, (((0,), (0,)), ((), ())), preferred_e...  62.3 us
  transfers between devices with their start and end apart: 9, of which 6 were waited for; matrix products, arithmetic and copies ran while one was open for 24% of the time, Pallas kernels for 0%

commit v1 on v0

--- a/solution.py
+++ b/solution.py
@@ -20,6 +20,27 @@
 adam_eps = 1e-08
 beta_first = 0.5
 beta_second = 0.5
+
+
+def ring_gather(value, axis, dim):
+    length, place, rows = (lax.axis_size(axis), lax.axis_index(axis), value.shape[dim])
+    upward = [(i, (i + 1) % length) for i in range(length)]
+    left = [(i, (i - 1) % length) for i in range(length)]
+    out = jnp.zeros((*value.shape[:dim], length * rows, *value.shape[dim + 1 :]), value.dtype)
+    out = lax.dynamic_update_slice_in_dim(out, value, place * rows, axis=dim)
+    from_left = from_right = value
+    halfway = length // 2
+    for step in range(1, halfway + 1):
+        from_left = lax.ppermute(from_left, axis, upward)
+        out = lax.dynamic_update_slice_in_dim(
+            out, from_left, (place - step) % length * rows, axis=dim
+        )
+        if step < length - halfway:
+            from_right = lax.ppermute(from_right, axis, left)
+            out = lax.dynamic_update_slice_in_dim(
+                out, from_right, (place + step) % length * rows, axis=dim
+            )
+    return out
 
 
 def to_low(value):
@@ -221,7 +242,7 @@
     total_count = lax.psum(jnp.sum(group_items.astype(jnp.float32)), "grp")
     masked = total_count * (L - K)
     copies = (
-        lax.all_gather(to_low(enc_cols), "dp", axis=0, tiled=True),
+        ring_gather(to_low(enc_cols), "dp", 0),
         lax.all_gather(to_low(enc_rows), "dp", axis=0, tiled=True),
         lax.all_gather(to_low(dec_cols), "dp", axis=0, tiled=True),
         lax.all_gather(to_low(dec_rows), "dp", axis=0, tiled=True),

time: 1730 us -> 1830 us (1.058)
  waiting for transfers between devices: 892 us -> 962 us
  local copies, waits for them, and re-layouts: 157 us -> 177 us
    ppermute x0 -> x7, waiting for transfers between devices: none -> 241 us  [the longest x4 169 us: ring_gather(): from_left = lax.ppermute(from_left, axis, upward)]
    all_gather x1 -> x0, waiting for transfers between devices: 141 us -> none  [body(): lax.all_gather(to_low(enc_cols), 'dp', axis=0, tiled=True)]
    all_gather x1, waiting for transfers between devices: 28.3 us -> 0.01 us  [body(): lax.all_gather(to_low(enc_rows), 'dp', axis=0, tiled=True)]
    convert_element_type x8 -> x7, other arithmetic: 48.9 us -> 43.7 us  [to_low(): return value.astype(jnp.bfloat16)]
  transfers between devices with their start and end apart: 9 -> 15, of which waited for: 6 -> 8; matrix products, arithmetic and copies ran while one was open for 24% -> 24% of each run, Pallas kernels for 0% -> 0%
where the time goes in v1:
time: 1830 us; the launch traced here: 1820 us
  waiting for transfers between devices  962 us (53%)
  matrix products  312 us (17%)
  other arithmetic  265 us (14%)
  local copies, waits for them, and re-layouts  177 us (10%)
  blocking collectives  67.7 us (4%)
  between operations  26 us (1%)
    reduce_scatter x1, waiting for transfers between devices, body(): lax.psum_scatter(grads[1], 'dp', scatter_dimension=0, tiled=True)  323 us
    reduce_scatter x1, waiting for transfers between devices, body(): lax.psum_scatter(grads[0], 'dp', scatter_dimension=0, tiled=True)  316 us
    ppermute x4, waiting for transfers between devices, ring_gather(): from_left = lax.ppermute(from_left, axis, upward)  169 us
    psum x1, waiting for transfers between devices, body(): lax.psum(shards[0].astype(jnp.bfloat16), 'grp').astype(jnp.float32)  81.2 us
    ppermute x3, waiting for transfers between devices, ring_gather(): from_right = lax.ppermute(from_right, axis, left)  72.1 us
    dot_general x11, matrix products, project(): jnp.einsum('...n,nm->...m', inputs, matrix, preferred_element_type=jnp.fl...  70.2 us
    dot_general x10, matrix products, project_back(): jnp.einsum('...m,nm->...n', grads, matrix, preferred_element_type=jnp.flo...  68.6 us
    scatter-add x1, other arithmetic, body(): dec_input = dec_input.at[item_rows, keep_rows].add(latent)  65.5 us
  transfers between devices with their start and end apart: 15, of which 8 were waited for; matrix products, arithmetic and copies ran while one was open for 24% of the time, Pallas kernels for 0%

profile of v1, /device:TPU:0, one launch (start us, length us, event | category | flops | bytes accessed | tf_op | source)
XLA Modules:
  0.0 1820.8 jit_solution(11735986431292530399)
XLA Ops:
  13.5 6.9 broadcast_in_dim.52
  23.6 4.4 collective-permute-start.1
  32.8 10.9 gather_fusion.2
  46.1 10.9 gather_fusion
  57.0 10.3 broadcast_select_fusion
  71.7 46.5 %collective-permute-done = bf16[128,8192]{1,0:T(8,128)(2,1)} collective-permute-done((bf16[128,8192]{1,0:T(8,128)(2,1)}, bf16[128,8192]{1,0:T(8,128)(2,1)}, u32[]{:S(2)}, u32[]{:S(2)}) %collective-permute-start) | collective-permute-done | bytes 2097184 | tf_op jit(solution)/shard_map/ppermute | solution.py:34
  118.8 11.9 psum.63
  130.7 7.8 mul.720
  138.5 8.4 slice.161
  146.9 10.4 gather_fusion.3
  158.0 24.0 %scatter_fusion = f32[8,256]{1,0:T(8,128)S(1)} fusion(f32[8,256]{1,0:T(8,128)S(1)} %broadcast_in_dim.55, s32[512]{0:T(512)S(1)} %reshape.496, f32[512]{0:T(512)S(1)} %broadcast.514), kind=kCustom, calls=%fused_computation.5 | custom fusion | bytes 10240 | tf_op jit(solution)/shard_map/scatter | solution.py:273
  187.3 4.6 slice_add_fusion
  201.0 59.8 %collective-permute-done.3 = bf16[128,8192]{1,0:T(8,128)(2,1)S(1)} collective-permute-done((bf16[128,8192]{1,0:T(8,128)(2,1)}, bf16[128,8192]{1,0:T(8,128)(2,1)S(1)}, u32[]{:S(2)}, u32[]{:S(2)}) %collective-permute-start.3) | collective-permute-done | bytes 2097184 | tf_op jit(solution)/shard_map/ppermute | solution.py:39
  265.9 59.1 %collective-permute-done.4 = bf16[128,8192]{1,0:T(8,128)(2,1)S(1)} collective-permute-done((bf16[128,8192]{1,0:T(8,128)(2,1)S(1)}, bf16[128,8192]{1,0:T(8,128)(2,1)S(1)}, u32[]{:S(2)}, u32[]{:S(2)}) %collective-permute-start.4) | collective-permute-done | bytes 2097184 | tf_op jit(solution)/shard_map/ppermute | solution.py:34
  328.3 12.3 collective-permute-done.5
  342.1 63.6 %collective-permute-done.6 = bf16[128,8192]{1,0:T(8,128)(2,1)S(1)} collective-permute-done((bf16[128,8192]{1,0:T(8,128)(2,1)S(1)}, bf16[128,8192]{1,0:T(8,128)(2,1)S(1)}, u32[]{:S(2)}, u32[]{:S(2)}) %collective-permute-start.6) | collective-permute-done | bytes 2097184 | tf_op jit(solution)/shard_map/ppermute | solution.py:34
  407.2 9.7 fusion.120
  417.4 6.9 fusion.23
  447.5 10.8 multiply_convert_fusion.2
  458.9 4.6 fusion.122
  467.2 65.5 %scatter_fusion.1 = f32[8,256,512]{2,1,0:T(8,128)} fusion(f32[8,256,512]{2,1,0:T(8,128)} %slice_add_fusion, s32[512]{0:T(512)S(1)} %reshape.496, f32[512,512]{1,0:T(8,128)} %bitcast.272), kind=kCustom, calls=%fused_computation.6 | custom fusion | flops 262144 | bytes 3149824 | tf_op jit(solution)/shard_map/scatter-add | solution.py:275
  538.7 6.3 convolution_convert_fusion
  553.0 4.5 copy.91
  557.5 14.6 multiply_reduce_fusion.1
  572.1 13.8 exponential_reduce_fusion
  586.0 15.5 fusion.42
  601.5 4.4 fusion.123
  608.2 9.3 multiply_convert_fusion.1
  617.6 4.6 fusion.124
  630.1 6.7 divide_convert_fusion
  636.8 6.6 multiply_reduce_fusion.4
  645.6 14.0 fusion.6
  659.6 7.1 convolution_bitcast_fusion.5
  666.7 6.7 multiply_reduce_fusion.5
  684.1 15.9 fusion.45
  700.0 23.3 %multiply_reduce_fusion = (f32[8,16,256]{2,1,0:T(8,128)S(1)}, f32[8,16,256,256]{2,3,1,0:T(8,128)}) fusion(f32[8,16,256,256]{2,3,1,0:T(8,128)} %get-tuple-element.109, f32[8,16,256]{2,1,0:T(8,128)S(1)} %log_add_fusion, bf16[8,256,16,32]{1,3,2,0:T(8,128)(2,1)} %bitcast.251, bf16[8,256,16,32]{1,3,2,0:T(8,128)(2,1)S(1)} %bitcast.249), kind=kOutput, calls=%fused_computation.10 | convolution fusion | flops 570392576 | bytes 71565312 | tf_op jit(solution)/shard_map/bqhe,bkhe->bhqk/dot_general | solution.py:171
  723.3 28.0 %multiply_convert_fusion = bf16[8,16,256,256]{2,3,1,0:T(8,128)(2,1)} fusion(f32[8,16,256,256]{2,3,1,0:T(8,128)} %get-tuple-element.121, f32[8,16,256,256]{2,3,1,0:T(8,128)} %get-tuple-element.109, f32[8,16,256]{2,1,0:T(8,128)S(1)} %get-tuple-element.120, f32[8,16,256]{2,1,0:T(8,128)S(1)} %log_add_fusion), kind=kLoop, calls=%fused_computation.9 | loop fusion | flops 41943040 | bytes 84148224 | tf_op jit(solution)/shard_map/convert_element_type | solution.py:47
  751.4 12.0 multiply_convert_fusion.6
  763.4 10.5 multiply_convert_fusion.7
  784.5 7.8 convolution_bitcast_fusion.3
  797.5 8.2 multiply_reduce_fusion.6
  820.4 4.6 convolution_bitcast_fusion.4
  834.2 11.0 fusion.16
  845.3 9.7 multiply_reduce_fusion.19
  861.8 5.5 convolution_convert_fusion.1
  869.4 4.6 multiply_reduce_fusion.7
  879.7 4.1 reshape.460
  890.3 6.3 convolution_bitcast_fusion.6
  896.7 7.0 convolution_bitcast_fusion.2
  903.7 8.6 convolution_bitcast_fusion.1
  912.3 22.9 %pad_maximum_fusion = f32[1024,8192]{1,0:T(8,128)} fusion(f32[1024,4096]{1,0:T(8,128)} %convolution_bitcast_fusion.1, f32[1024,1024]{1,0:T(8,128)} %convolution_bitcast_fusion.6, f32[1024,3072]{1,0:T(8,128)} %convolution_bitcast_fusion.2), kind=kLoop, calls=%fused_computation.7 | loop fusion | flops 16777216 | bytes 67108864 | tf_op jit(solution)/shard_map/concatenate | solution.py:202
  935.4 4.6 copy.152
  940.1 6.9 multiply_reduce_fusion.20
  947.8 4.7 fusion.125
  952.5 8.8 convolution_bitcast_fusion
  961.3 18.8 %pad_maximum_fusion.1 = f32[8192,1024]{1,0:T(8,128)} fusion(f32[4096,1024]{1,0:T(8,128)S(1)} %fusion.125, f32[4096,1024]{1,0:T(8,128)} %convolution_bitcast_fusion), kind=kLoop, calls=%fused_computation.8 | loop fusion | flops 8388608 | bytes 67108864 | tf_op jit(solution)/shard_map/concatenate | solution.py:308
  984.6 316.3 %reduce-scatter.5.cloned.1.call-done = f32[128,8192]{1,0:T(8,128)} async-done(((f32[1024,8192]{1,0:T(8,128)}), f32[128,8192]{1,0:T(8,128)}) %reduce-scatter.5.cloned.1.call-update) | async-done | bytes 4194320 | tf_op jit(solution)/shard_map/reduce_scatter | solution.py:315
  1304.7 322.6 %reduce-scatter.7.cloned.1.call-done = f32[1024,1024]{1,0:T(8,128)} async-done(((f32[8192,1024]{1,0:T(8,128)}), f32[1024,1024]{1,0:T(8,128)}) %reduce-scatter.7.cloned.1.call-update) | async-done | bytes 4194320 | tf_op jit(solution)/shard_map/reduce_scatter | solution.py:316
  1632.3 38.8 %all-reduce = (f32[6,1024]{1,0:T(8,128)S(1)}, f32[7,512]{1,0:T(8,128)S(1)}, f32[]{:T(128)}) all-reduce(f32[6,1024]{1,0:T(8,128)S(1)} %concatenate.37, f32[7,512]{1,0:T(8,128)S(1)} %concatenate.38, f32[]{:T(128)} %get-tuple-element.69), channel_id=1, replica_groups=mesh['grp'=4,'dp'=8] {'grp','dp'}, use_global_device_ids=true, to_apply=%region_54.55 | all-reduce | flops 9729 | bytes 77832 | tf_op jit(solution)/shard_map/psum | solution.py:326
  1672.3 81.2 %all-reduce.4.cloned.1.call-done = (bf16[128,8192]{1,0:T(8,128)(2,1)}, bf16[1024,1024]{1,0:T(8,128)(2,1)}, bf16[64,4096]{1,0:T(8,128)(2,1)}, bf16[512,512]{1,0:T(8,128)(2,1)}) async-done(((bf16[128,8192]{1,0:T(8,128)(2,1)}, bf16[1024,1024]{1,0:T(8,128)(2,1)}, bf16[64,4096]{1,0:T(8,128)(2,1)}, bf16[512,512]{1,0:T(8,128)(2,1)}), (bf16[128,8192]{1,0:T(8,128)(2,1)}, bf16[1024,1024]{1,0:T(8,128)(2,1)}, ...) | async-done | bytes 5242896 | tf_op jit(solution)/shard_map/psum | solution.py:321
  1765.7 17.0 psum.68
  1790.0 4.2 fusion.64
  1795.1 8.9 fusion.35
  1805.9 5.6 fusion.30
  (440 shorter events, 202.7 us)
Async XLA Ops:
  7.2 39.0 %copy-start = (f32[1,512,1536]{2,1,0:T(8,128)S(1)}, f32[1,512,1536]{2,1,0:T(8,128)}, u32[]{:S(2)}) copy-start(f32[1,512,1536]{2,1,0:T(8,128)} %param.29) | copy-start | bytes 9437188
  7.2 400.0 %all-gather.4.cloned.1.call-start = ((), (), s32[]{:S(2)}) async-start(), calls=%async_computation.4 | async-start | bytes 18874368 | tf_op jit(solution)/shard_map/all_gather | solution.py:246
  11.3 452.6 %all-gather.6.cloned.1.call-start = ((), (), s32[]{:S(2)}) async-start(), calls=%async_computation.5 | async-start | bytes 4718592 | tf_op jit(solution)/shard_map/all_gather | solution.py:248
  13.4 524.7 %all-gather.8.cloned.1.call-start = ((), (), s32[]{:S(2)}) async-start(), calls=%async_computation.6 | async-start | bytes 4718592 | tf_op jit(solution)/shard_map/all_gather | solution.py:247
  23.1 95.2 %collective-permute-start = (bf16[128,8192]{1,0:T(8,128)(2,1)}, bf16[128,8192]{1,0:T(8,128)(2,1)}, u32[]{:S(2)}, u32[]{:S(2)}) collective-permute-start(bf16[128,8192]{1,0:T(8,128)(2,1)} %get-tuple-element.76), channel_id=1, source_target_pairs={{0,1},{1,2},{2,3},{3,4},{4,5},{5,6},{6,7},{7,0},{8,9},{9,10},{10,1... | collective-permute-start | bytes 6291464 | tf_op jit(solution)/shard_map/ppermute | solution.py:34
  23.6 168.3 %collective-permute-start.1 = (bf16[128,8192]{1,0:T(8,128)(2,1)}, bf16[128,8192]{1,0:T(8,128)(2,1)}, u32[]{:S(2)}, u32[]{:S(2)}) collective-permute-start(bf16[128,8192]{1,0:T(8,128)(2,1)} %get-tuple-element.76), channel_id=1, source_target_pairs={{0,7},{1,0},{2,1},{3,2},{4,3},{5,4},{6,5},{7,6},{8,15},{9,8},{10,9... | collective-permute-start | bytes 6291464 | tf_op jit(solution)/shard_map/ppermute | solution.py:39
  28.8 951.4 %reduce-scatter.9.cloned.1.call-start = ((), (), s32[]{:S(2)}) async-start(), calls=%async_computation.9 | async-start | bytes 9437184 | tf_op jit(solution)/shard_map/reduce_scatter | solution.py:317
  29.0 117.8 %copy-start.6 = (s32[512]{0:T(512)}, s32[512]{0:T(512)S(1)}, u32[]{:S(2)}) copy-start(s32[512]{0:T(512)S(1)} %reshape.472) | copy-start | bytes 6148
  32.7 374.5 %copy-start.109 = (pred[8,64]{1,0:T(8,128)(4,1)}, pred[8,64]{1,0:T(8,128)(4,1)S(1)}, u32[]{:S(2)}) copy-start(pred[8,64]{1,0:T(8,128)(4,1)S(1)} %get-tuple-element.74) | copy-start | bytes 1540
  57.0 10.3 copy-start.52
  118.2 76.5 %collective-permute-start.2 = (bf16[128,8192]{1,0:T(8,128)(2,1)}, bf16[128,8192]{1,0:T(8,128)(2,1)S(1)}, u32[]{:S(2)}, u32[]{:S(2)}) collective-permute-start(bf16[128,8192]{1,0:T(8,128)(2,1)} %collective-permute-done), channel_id=1, source_target_pairs={{0,1},{1,2},{2,3},{3,4},{4,5},{5,6},{6,7},{7,0},{8,9},{9,10},{10,1... | collective-permute-start | bytes 6291464 | tf_op jit(solution)/shard_map/ppermute | solution.py:34
  158.0 27.1 %copy-start.79 = (f32[7,512]{1,0:T(8,128)S(1)}, f32[7,512]{1,0:T(8,128)}, u32[]{:S(2)}) copy-start(f32[7,512]{1,0:T(8,128)} %param.37) | copy-start | bytes 43012
  185.7 352.4 %copy-start.106 = (f32[1,512]{1,0:T(1,128)}, f32[1,512]{1,0:T(1,128)S(1)}, u32[]{:S(2)}) copy-start(f32[1,512]{1,0:T(1,128)S(1)} %get-tuple-element.93) | copy-start | bytes 6148
  185.7 352.4 %copy-start.121 = (f32[1,512]{1,0:T(1,128)}, f32[1,512]{1,0:T(1,128)S(1)}, u32[]{:S(2)}) copy-start(f32[1,512]{1,0:T(1,128)S(1)} %get-tuple-element.92) | copy-start | bytes 6148
  185.8 231.6 %copy-start.64 = (f32[1,1024]{1,0:T(1,128)}, f32[1,1024]{1,0:T(1,128)S(1)}, u32[]{:S(2)}) copy-start(f32[1,1024]{1,0:T(1,128)S(1)} %get-tuple-element.87) | copy-start | bytes 12292
  185.8 231.6 %copy-start.68 = (f32[1,1024]{1,0:T(1,128)}, f32[1,1024]{1,0:T(1,128)S(1)}, u32[]{:S(2)}) copy-start(f32[1,1024]{1,0:T(1,128)S(1)} %get-tuple-element.86) | copy-start | bytes 12292
  185.8 261.6 %copy-start.93 = (f32[1,1024]{1,0:T(1,128)}, f32[1,1024]{1,0:T(1,128)S(1)}, u32[]{:S(2)}) copy-start(f32[1,1024]{1,0:T(1,128)S(1)} %get-tuple-element.85) | copy-start | bytes 12292
  185.8 261.6 %copy-start.115 = (f32[1,1024]{1,0:T(1,128)}, f32[1,1024]{1,0:T(1,128)S(1)}, u32[]{:S(2)}) copy-start(f32[1,1024]{1,0:T(1,128)S(1)} %get-tuple-element.84) | copy-start | bytes 12292
  185.8 278.1 %copy-start.100 = (f32[1,1024]{1,0:T(1,128)}, f32[1,1024]{1,0:T(1,128)S(1)}, u32[]{:S(2)}) copy-start(f32[1,1024]{1,0:T(1,128)S(1)} %get-tuple-element.83) | copy-start | bytes 12292
  185.8 278.1 %copy-start.117 = (f32[1,1024]{1,0:T(1,128)}, f32[1,1024]{1,0:T(1,128)S(1)}, u32[]{:S(2)}) copy-start(f32[1,1024]{1,0:T(1,128)S(1)} %get-tuple-element.88) | copy-start | bytes 12292
  191.9 68.9 %collective-permute-start.3 = (bf16[128,8192]{1,0:T(8,128)(2,1)}, bf16[128,8192]{1,0:T(8,128)(2,1)S(1)}, u32[]{:S(2)}, u32[]{:S(2)}) collective-permute-start(bf16[128,8192]{1,0:T(8,128)(2,1)} %collective-permute-done.1), channel_id=1, source_target_pairs={{0,7},{1,0},{2,1},{3,2},{4,3},{5,4},{6,5},{7,6},{8,15},{9,8},{10,9... | collective-permute-start | bytes 6291464 | tf_op jit(solution)/shard_map/ppermute | solution.py:39
  194.8 130.2 %collective-permute-start.4 = (bf16[128,8192]{1,0:T(8,128)(2,1)S(1)}, bf16[128,8192]{1,0:T(8,128)(2,1)S(1)}, u32[]{:S(2)}, u32[]{:S(2)}) collective-permute-start(bf16[128,8192]{1,0:T(8,128)(2,1)S(1)} %collective-permute-done.2), channel_id=1, source_target_pairs={{0,1},{1,2},{2,3},{3,4},{4,5},{5,6},{6,7},{7,0},{8,9},{9,10},{10,1... | collective-permute-start | bytes 6291464 | tf_op jit(solution)/shard_map/ppermute | solution.py:34
  260.8 79.8 %collective-permute-start.5 = (bf16[128,8192]{1,0:T(8,128)(2,1)S(1)}, bf16[128,8192]{1,0:T(8,128)(2,1)S(1)}, u32[]{:S(2)}, u32[]{:S(2)}) collective-permute-start(bf16[128,8192]{1,0:T(8,128)(2,1)S(1)} %collective-permute-done.3), channel_id=1, source_target_pairs={{0,7},{1,0},{2,1},{3,2},{4,3},{5,4},{6,5},{7,6},{8,15},{9,8},{10,9... | collective-permute-start | bytes 6291464 | tf_op jit(solution)/shard_map/ppermute | solution.py:39
  325.0 80.7 %collective-permute-start.6 = (bf16[128,8192]{1,0:T(8,128)(2,1)S(1)}, bf16[128,8192]{1,0:T(8,128)(2,1)S(1)}, u32[]{:S(2)}, u32[]{:S(2)}) collective-permute-start(bf16[128,8192]{1,0:T(8,128)(2,1)S(1)} %collective-permute-done.4), channel_id=1, source_target_pairs={{0,1},{1,2},{2,3},{3,4},{4,5},{5,6},{6,7},{7,0},{8,9},{9,10},{10,1... | collective-permute-start | bytes 6291464 | tf_op jit(solution)/shard_map/ppermute | solution.py:34
  416.9 26.3 %copy-start.17 = (f32[8,64,1024]{2,1,0:T(8,128)}, f32[8,64,1024]{2,1,0:T(8,128)S(1)}, u32[]{:S(2)}) copy-start(f32[8,64,1024]{2,1,0:T(8,128)S(1)} %get-tuple-element.99) | copy-start | bytes 6291460
  447.0 11.3 copy-start.23
  447.0 11.2 copy-start.81
  447.0 11.3 slice-start
  447.4 10.9 copy-start.95
  447.4 10.9 slice-start.1
  447.4 10.9 slice-start.2
  447.4 11.4 slice-start.3
  463.4 69.2 %copy-start.38 = (f32[8,64,1024]{2,1,0:T(8,128)}, f32[8,64,1024]{2,1,0:T(8,128)S(1)}, u32[]{:S(2)}) copy-start(f32[8,64,1024]{2,1,0:T(8,128)S(1)} %get-tuple-element.107) | copy-start | bytes 6291460
  463.4 69.2 %copy-start.83 = (f32[8,64]{1,0:T(8,128)}, f32[8,64]{1,0:T(8,128)S(1)}, u32[]{:S(2)}) copy-start(f32[8,64]{1,0:T(8,128)S(1)} %broadcast_multiply_fusion.20) | copy-start | bytes 6148
  463.8 68.9 %copy-start.102 = (f32[8,64]{1,0:T(8,128)}, f32[8,64]{1,0:T(8,128)S(1)}, u32[]{:S(2)}) copy-start(f32[8,64]{1,0:T(8,128)S(1)} %add_rsqrt_fusion.4) | copy-start | bytes 6148
  553.0 19.1 %copy-start.13 = (bf16[8,256,512]{1,2,0:T(8,128)(2,1)}, bf16[8,256,512]{1,2,0:T(8,128)(2,1)S(1)}, u32[]{:S(2)}) copy-start(bf16[8,256,512]{1,2,0:T(8,128)(2,1)S(1)} %copy.92) | copy-start | bytes 6291460
  572.1 13.9 copy-start.19
  608.2 9.4 copy-start.130
  622.2 21.3 %copy-start.28 = (f32[8,256,512]{2,1,0:T(8,128)}, f32[8,256,512]{2,1,0:T(8,128)S(1)}, u32[]{:S(2)}) copy-start(f32[8,256,512]{2,1,0:T(8,128)S(1)} %get-tuple-element.115) | copy-start | bytes 12582916
  622.2 21.2 %copy-start.77 = (f32[8,256]{1,0:T(8,128)}, f32[8,256]{1,0:T(8,128)S(1)}, u32[]{:S(2)}) copy-start(f32[8,256]{1,0:T(8,128)S(1)} %broadcast_multiply_fusion.11) | copy-start | bytes 24580
  623.1 20.4 %copy-start.91 = (f32[8,256]{1,0:T(8,128)}, f32[8,256]{1,0:T(8,128)S(1)}, u32[]{:S(2)}) copy-start(f32[8,256]{1,0:T(8,128)S(1)} %add_rsqrt_fusion.1) | copy-start | bytes 24580
  645.0 28.4 %copy-start.26 = (f32[8,256,512]{2,1,0:T(8,128)}, f32[8,256,512]{2,1,0:T(8,128)S(1)}, u32[]{:S(2)}) copy-start(f32[8,256,512]{2,1,0:T(8,128)S(1)} %subtract_multiply_fusion) | copy-start | bytes 12582916
  723.3 28.0 %copy-start.14 = (bf16[8,256,512]{1,2,0:T(8,128)(2,1)S(1)}, bf16[8,256,512]{1,2,0:T(8,128)(2,1)}, u32[]{:S(2)}) copy-start(bf16[8,256,512]{1,2,0:T(8,128)(2,1)} %copy-done.13) | copy-start | bytes 6291460
  795.9 9.8 copy-start.4
  795.9 186.6 %reduce-scatter.11.cloned.1.call-start = ((), (), s32[]{:S(2)}) async-start(), calls=%async_computation.10 | async-start | bytes 9437184 | tf_op jit(solution)/shard_map/reduce_scatter | solution.py:318
  828.9 472.0 %reduce-scatter.5.cloned.1.call-start = ((), (), s32[]{:S(2)}) async-start(), calls=%async_computation.7 | async-start | bytes 37748736 | tf_op jit(solution)/shard_map/reduce_scatter | solution.py:315
  834.1 20.9 %copy-start.41 = (f32[8,64,1024]{2,1,0:T(8,128)}, f32[8,64,1024]{2,1,0:T(8,128)S(1)}, u32[]{:S(2)}) copy-start(f32[8,64,1024]{2,1,0:T(8,128)S(1)} %subtract_multiply_fusion.4) | copy-start | bytes 6291460
  834.2 11.1 copy-start.24
  834.2 11.1 copy-start.82
  834.2 11.1 copy-start.94
  834.2 11.1 copy-start.96
  845.3 9.7 copy-start.135
  935.2 692.1 %reduce-scatter.7.cloned.1.call-start = ((), (), s32[]{:S(2)}) async-start(), calls=%async_computation.8 | async-start | bytes 37748736 | tf_op jit(solution)/shard_map/reduce_scatter | solution.py:316
  980.1 773.4 %all-reduce.4.cloned.1.call-start = ((), (), s32[]{:S(2)}) async-start(), calls=%async_computation.11 | async-start | bytes 10485760 | tf_op jit(solution)/shard_map/psum | solution.py:321
  1631.2 153.5 %copy-start.80 = (f32[7,512]{1,0:T(8,128)S(1)}, f32[7,512]{1,0:T(8,128)}, u32[]{:S(2)}) copy-start(f32[7,512]{1,0:T(8,128)} %param.37) | copy-start | bytes 43012
  1631.2 153.5 %copy-start.97 = (f32[7,512]{1,0:T(8,128)S(1)}, f32[7,512]{1,0:T(8,128)}, u32[]{:S(2)}) copy-start(f32[7,512]{1,0:T(8,128)} %param.43) | copy-start | bytes 43012
  1631.3 153.5 %copy-start.98 = (f32[7,512]{1,0:T(8,128)S(1)}, f32[7,512]{1,0:T(8,128)}, u32[]{:S(2)}) copy-start(f32[7,512]{1,0:T(8,128)} %param.49) | copy-start | bytes 43012
  1631.3 154.2 %copy-start.72 = (f32[6,1024]{1,0:T(8,128)S(1)}, f32[6,1024]{1,0:T(8,128)}, u32[]{:S(2)}) copy-start(f32[6,1024]{1,0:T(8,128)} %param.36) | copy-start | bytes 73732
  1631.3 154.2 %copy-start.88 = (f32[6,1024]{1,0:T(8,128)S(1)}, f32[6,1024]{1,0:T(8,128)}, u32[]{:S(2)}) copy-start(f32[6,1024]{1,0:T(8,128)} %param.42) | copy-start | bytes 73732
  1631.3 154.1 %copy-start.89 = (f32[6,1024]{1,0:T(8,128)S(1)}, f32[6,1024]{1,0:T(8,128)}, u32[]{:S(2)}) copy-start(f32[6,1024]{1,0:T(8,128)} %param.48) | copy-start | bytes 73732
  1631.3 154.8 %copy-start.50 = (f32[512,512]{1,0:T(8,128)S(1)}, f32[512,512]{1,0:T(8,128)}, u32[]{:S(2)}) copy-start(f32[512,512]{1,0:T(8,128)} %param.35) | copy-start | bytes 3145732
  1795.1 8.9 copy-start.44
  1795.1 9.1 copy-start.54
  1795.1 10.8 copy-start.55
  (94 other events, 429.7 us)
Sparse Core Ops, SparseCore 0:
  11.4 235.4 all-gather.3
  249.1 77.5 all-gather.5
  328.8 67.1 all-gather.7
  796.0 88.5 reduce-scatter.8
  886.8 87.9 reduce-scatter.10
  977.0 323.8 reduce-scatter.4
  1303.4 323.8 reduce-scatter.6
  1632.2 121.2 all-reduce.3
